TPU v7x, 32 devices: a whole 2x2x4 slice. The times are simulated.
32 devices in a mesh: row: 4 (over z), col: 8 (over y, x, core).
Axes of the slice: x: 2, y: 2, z: 4, core: 2. Of those that a mesh axis runs over, the one named last changes fastest.
Arguments:
- state_start: bfloat16 [512, 2048], P('row', 'col'), may hold values from -360 to 360
- actions: int32 [512, 2], P('row'), may hold values from 0 to 17
- targets: bfloat16 [2, 512, 2048], P(None, 'row'), may hold values from -504 to 504
- w_in: bfloat16 [2048, 4096], P('row', 'col'), may hold values from -0.125 to 0.125
- w_out: bfloat16 [4096, 2048], P('col', 'row'), may hold values from -0.09375 to 0.09375
- action_embed: bfloat16 [18, 4096], P(None, 'col'), may hold values from -6 to 6
Outputs:
- grad_w_in: float32 [2048, 4096], P('row', 'col')
- grad_w_out: float32 [4096, 2048], P('col', 'row')
All inputs are finite; a program needn't handle non-finite values.
Results may differ from a plain program's by a relative error of at most 0.035.
Values may be sent and summed in bfloat16 or wider, within the bound.
A program may use at most 64 MiB of HBM per device.

v0:
```python
import jax
import jax.numpy as jnp
from jax import lax
from jax.sharding import PartitionSpec as P

EPS = 1e-06
LOSS_SCALE = 128.0


def silu_grad(pre_act):
    gate_val = jax.nn.sigmoid(pre_act)
    return gate_val * (1.0 + pre_act * (1.0 - gate_val))


def cosine_from(state_f, target_f, self_dot, cross_dot, target_dot):
    inv_state = lax.rsqrt(self_dot + EPS)
    inv_target = lax.rsqrt(target_dot + EPS)
    cosine = cross_dot * inv_state * inv_target
    return -LOSS_SCALE * (
        target_f * inv_state * inv_target - cosine * state_f * inv_state * inv_state
    )


def shared_cosine(state, target):
    state_f = state.astype(jnp.float32)
    target_f = target.astype(jnp.float32)
    self_dot, cross_dot, target_dot = lax.psum(
        (
            jnp.sum(state_f * state_f, axis=-1),
            jnp.sum(state_f * target_f, axis=-1),
            jnp.sum(target_f * target_f, axis=-1),
        ),
        "col",
    )
    return cosine_from(
        state_f, target_f, self_dot[:, None], cross_dot[:, None], target_dot[:, None]
    )


def on_device(state_start, actions, targets, w_in, w_out, action_embed):
    unroll_steps = targets.shape[0]
    col_width = state_start.shape[1]
    w_in_panel = lax.all_gather(w_in, "row", axis=0, tiled=True)
    w_out_panel = lax.all_gather(w_out, "row", axis=1, tiled=True)
    col_start = lax.axis_index("col") * col_width
    action_ids = jnp.arange(action_embed.shape[0], dtype=jnp.int32)
    contract_last = (((1,), (1,)), ((), ()))
    current = state_start
    full_states = []
    pre_list = []
    hidden_list = []
    cos_terms = []
    for unroll in range(unroll_steps):
        full_rows = lax.all_gather(current, "col", axis=1, tiled=True)
        onehot = (actions[:, unroll][:, None] == action_ids[None, :]).astype(jnp.bfloat16)
        pre_act = jnp.dot(full_rows, w_in_panel, preferred_element_type=jnp.float32) + jnp.dot(
            onehot, action_embed, preferred_element_type=jnp.float32
        )
        hidden = jax.nn.silu(pre_act).astype(jnp.bfloat16)
        partial_value = jnp.dot(hidden, w_out_panel, preferred_element_type=jnp.float32)
        target = targets[unroll]
        branch = lax.psum_scatter(
            partial_value.astype(jnp.bfloat16), "col", scatter_dimension=1, tiled=True
        ).astype(jnp.float32)
        current = (current.astype(jnp.float32) + branch).astype(jnp.bfloat16)
        target_slice = lax.dynamic_slice_in_dim(target, col_start, col_width, 1)
        cos_terms.append(shared_cosine(current, target_slice))
        full_states.append(full_rows)
        pre_list.append(pre_act)
        hidden_list.append(hidden)
    state_grad = cos_terms[unroll_steps - 1].astype(jnp.bfloat16)
    grad_list = [None] * unroll_steps
    hid_grads = [None] * unroll_steps
    for unroll in reversed(range(unroll_steps)):
        grad_rows = lax.all_gather(state_grad, "col", axis=1, tiled=True)
        back = lax.dot_general(
            grad_rows, w_out_panel, contract_last, preferred_element_type=jnp.float32
        )
        hid_grad = (back * silu_grad(pre_list[unroll])).astype(jnp.bfloat16)
        grad_list[unroll] = grad_rows
        hid_grads[unroll] = hid_grad
        if unroll > 0:
            input_part = lax.dot_general(
                hid_grad, w_in_panel, contract_last, preferred_element_type=jnp.float32
            )
            summed = lax.psum_scatter(
                input_part.astype(jnp.bfloat16), "col", scatter_dimension=1, tiled=True
            ).astype(jnp.float32)
            state_grad = (state_grad.astype(jnp.float32) + summed + cos_terms[unroll - 1]).astype(
                jnp.bfloat16
            )
    grad_stack = jnp.stack(grad_list)
    hidden_stack = jnp.stack(hidden_list)
    state_stack = jnp.stack(full_states)
    hid_stack = jnp.stack(hid_grads)
    grad_feature_blocks = lax.all_to_all(grad_stack, "row", split_axis=2, concat_axis=1, tiled=True)
    hidden_all = lax.all_gather(hidden_stack, "row", axis=1, tiled=True)
    grad_w_out = jnp.einsum(
        "kbf,kbd->fd", hidden_all, grad_feature_blocks, preferred_element_type=jnp.float32
    )
    state_feature_blocks = lax.all_to_all(
        state_stack, "row", split_axis=2, concat_axis=1, tiled=True
    )
    hid_all = lax.all_gather(hid_stack, "row", axis=1, tiled=True)
    grad_w_in = jnp.einsum(
        "kbd,kbf->df", state_feature_blocks, hid_all, preferred_element_type=jnp.float32
    )
    return (grad_w_in, grad_w_out)


def solution(mesh):
    in_specs = (
        P("row", "col"),
        P("row", None),
        P(None, "row", None),
        P("row", "col"),
        P("col", "row"),
        P(None, "col"),
    )
    out_specs = (P("row", "col"), P("col", "row"))
    return jax.shard_map(
        on_device, mesh=mesh, in_specs=in_specs, out_specs=out_specs, check_vma=False
    )
```

profile of v0, /device:TPU:0, one launch (start us, length us, event | category | flops | bytes accessed | tf_op | source)
XLA Modules:
  0.0 336.0 jit_solution(11510671725148091114)
XLA Ops:
  8.7 12.7 %all_gather.24 = bf16[128,2048]{1,0:T(8,128)(2,1)S(1)} all-gather(bf16[128,256]{1,0:T(8,128)(2,1)} %param.6), channel_id=1, replica_groups=mesh['row'=4,'col'=8] {'col'}, dimensions={1}, use_global_device_ids=true | all-gather | bytes 589824 | tf_op jit(solution)/shard_map/all_gather | solution.py:54
  22.4 35.6 %all-gather.5.cloned.1.call-done = bf16[2048,512]{1,0:T(8,128)(2,1)} async-done(((bf16[512,512]{1,0:T(8,128)(2,1)}), bf16[2048,512]{1,0:T(8,128)(2,1)}) %all-gather.5.cloned.1.call-update) | async-done | bytes 2097168 | tf_op jit(solution)/shard_map/all_gather | solution.py:43
  58.0 2.0 convolution_add_fusion.1
  60.0 44.0 %all-gather.7.cloned.1.call-done = bf16[512,2048]{1,0:T(8,128)(2,1)} async-done(((bf16[512,512]{1,0:T(8,128)(2,1)}), bf16[512,2048]{1,0:T(8,128)(2,1)}) %all-gather.7.cloned.1.call-update) | async-done | bytes 2097168 | tf_op jit(solution)/shard_map/all_gather | solution.py:44
  104.0 2.9 convolution_convert_fusion.2
  107.9 2.1 fusion.29
  110.0 30.6 %reduce-scatter.4.cloned.1.call-done = bf16[128,256]{1,0:T(8,128)(2,1)} async-done(((bf16[128,2048]{1,0:T(8,128)(2,1)}), bf16[128,256]{1,0:T(8,128)(2,1)}) %reduce-scatter.4.cloned.1.call-update) | async-done | bytes 65552 | tf_op jit(solution)/shard_map/reduce_scatter | solution.py:62
  141.8 10.9 %all_gather.27 = bf16[128,2048]{1,0:T(8,128)(2,1)S(1)} all-gather(bf16[128,256]{1,0:T(8,128)(2,1)S(1)} %get-tuple-element.14), channel_id=1, replica_groups=mesh['row'=4,'col'=8] {'col'}, dimensions={1}, use_global_device_ids=true | all-gather | bytes 589824 | tf_op jit(solution)/shard_map/all_gather | solution.py:54
  152.7 2.1 convolution_add_fusion
  154.8 2.2 convolution_convert_fusion.1
  157.1 34.2 %reduce-scatter.6.cloned.1.call-done = bf16[128,256]{1,0:T(8,128)(2,1)} async-done(((bf16[128,2048]{1,0:T(8,128)(2,1)}), bf16[128,256]{1,0:T(8,128)(2,1)}) %reduce-scatter.6.cloned.1.call-update) | async-done | bytes 65552 | tf_op jit(solution)/shard_map/reduce_scatter | solution.py:62
  192.3 12.1 %all-reduce = (f32[128]{0:T(128)S(1)}, f32[128]{0:T(128)S(1)}, f32[128]{0:T(128)S(1)}, f32[128]{0:T(128)S(1)}, f32[128]{0:T(128)S(1)}, /*index=5*/f32[128]{0:T(128)S(1)}) all-reduce(f32[128]{0:T(128)S(1)} %get-tuple-element.5, f32[128]{0:T(128)S(1)} %get-tuple-element.6, ...), channel_id=1, replica_groups=mesh['row'=4,'col'=8] {'col'}, use_global_device_ids=true, to_apply=%region_7.8 | all-reduce | flops 768 | bytes 6144 | tf_op jit(solution)/shard_map/psum | solution.py:27
  206.1 10.9 %all_gather.28 = bf16[128,2048]{1,0:T(8,128)(2,1)S(1)} all-gather(bf16[128,256]{1,0:T(8,128)(2,1)S(1)} %fusion.8), channel_id=1, replica_groups=mesh['row'=4,'col'=8] {'col'}, dimensions={1}, use_global_device_ids=true | all-gather | bytes 589824 | tf_op jit(solution)/shard_map/all_gather | solution.py:75
  217.8 2.4 fusion
  222.6 2.0 copy.11
  224.6 4.9 %all-to-all-start = ((bf16[2,128,2048]{1,0,2:T(2,128)(2,1)}), bf16[2,128,2048]{1,0,2:T(2,128)(2,1)S(1)}, u32[]{:S(2)}, u32[]{:S(2)}) async-start(bf16[2,128,2048]{1,0,2:T(2,128)(2,1)} %copy.11), calls=%async_computation.1 | async-start | bytes 2097152 | tf_op jit(solution)/shard_map/all_to_all | solution.py:101
  231.4 25.5 %reduce-scatter.8.cloned.1.call-done = bf16[128,256]{1,0:T(8,128)(2,1)} async-done(((bf16[128,2048]{1,0:T(8,128)(2,1)}), bf16[128,256]{1,0:T(8,128)(2,1)}) %reduce-scatter.8.cloned.1.call-update) | async-done | bytes 65552 | tf_op jit(solution)/shard_map/reduce_scatter | solution.py:86
  258.0 10.9 %all_gather.29 = bf16[128,2048]{1,0:T(8,128)(2,1)S(1)} all-gather(bf16[128,256]{1,0:T(8,128)(2,1)S(1)} %fusion.16), channel_id=1, replica_groups=mesh['row'=4,'col'=8] {'col'}, dimensions={1}, use_global_device_ids=true | all-gather | bytes 589824 | tf_op jit(solution)/shard_map/all_gather | solution.py:75
  271.0 4.6 %all-to-all-start.1 = ((bf16[2,128,2048]{1,0,2:T(2,128)(2,1)}), bf16[2,128,2048]{1,0,2:T(2,128)(2,1)S(1)}, u32[]{:S(2)}, u32[]{:S(2)}) async-start(bf16[2,128,2048]{1,0,2:T(2,128)(2,1)} %copy.13), calls=%async_computation.4 | async-start | bytes 2097152 | tf_op jit(solution)/shard_map/all_to_all | solution.py:96
  275.6 2.5 fusion.2
  280.1 33.4 %all-to-all-done.1 = bf16[2,128,2048]{1,0,2:T(2,128)(2,1)S(1)} async-done(((bf16[2,128,2048]{1,0,2:T(2,128)(2,1)}), bf16[2,128,2048]{1,0,2:T(2,128)(2,1)S(1)}, u32[]{:S(2)}, u32[]{:S(2)}) %all-to-all-start.1) | async-done | bytes 1048608 | tf_op jit(solution)/shard_map/all_to_all | solution.py:96
  314.3 2.9 convolution_bitcast_fusion
  317.2 9.0 %all-gather.9.cloned.1.call-done = bf16[2,512,512]{2,1,0:T(8,128)(2,1)} async-done(((bf16[2,128,512]{2,1,0:T(8,128)(2,1)}), bf16[2,512,512]{2,1,0:T(8,128)(2,1)}) %all-gather.9.cloned.1.call-update) | async-done | bytes 1048592 | tf_op jit(solution)/shard_map/all_gather | solution.py:104
  326.2 2.9 convolution_bitcast_fusion.1
  (56 shorter events, 18.3 us)
Async XLA Ops:
  7.2 15.0 %copy-start = (bf16[18,512]{1,0:T(8,128)(2,1)S(1)}, bf16[18,512]{1,0:T(8,128)(2,1)}, u32[]{:S(2)}) copy-start(bf16[18,512]{1,0:T(8,128)(2,1)} %param.11) | copy-start | bytes 55300
  7.2 50.8 %all-gather.5.cloned.1.call-start = ((), (), s32[]{:S(2)}) async-start(), calls=%async_computation.5 | async-start | bytes 2621440 | tf_op jit(solution)/shard_map/all_gather | solution.py:43
  7.9 96.1 %all-gather.7.cloned.1.call-start = ((), (), s32[]{:S(2)}) async-start(), calls=%async_computation.6 | async-start | bytes 2621440 | tf_op jit(solution)/shard_map/all_gather | solution.py:44
  8.7 132.0 %reduce-scatter.4.cloned.1.call-start = ((), (), s32[]{:S(2)}) async-start(), calls=%async_computation.7 | async-start | bytes 589824 | tf_op jit(solution)/shard_map/reduce_scatter | solution.py:62
  106.9 45.8 %copy-start.1 = (bf16[2048,512]{1,0:T(8,128)(2,1)S(1)}, bf16[2048,512]{1,0:T(8,128)(2,1)}, u32[]{:S(2)}) copy-start(bf16[2048,512]{1,0:T(8,128)(2,1)} %all-gather.5.cloned.1.call-done) | copy-start | bytes 6291460
  106.9 84.4 %reduce-scatter.6.cloned.1.call-start = ((), (), s32[]{:S(2)}) async-start(), calls=%async_computation.8 | async-start | bytes 589824 | tf_op jit(solution)/shard_map/reduce_scatter | solution.py:62
  110.0 31.7 %copy-start.4 = (bf16[1,128,2048]{2,1,0:T(8,128)(2,1)}, bf16[1,128,2048]{2,1,0:T(8,128)(2,1)S(1)}, u32[]{:S(2)}) copy-start(bf16[1,128,2048]{2,1,0:T(8,128)(2,1)S(1)} %get-tuple-element.16) | copy-start | bytes 1572868
  140.6 14.2 %copy-start.9 = (bf16[512,2048]{1,0:T(8,128)(2,1)S(1)}, bf16[512,2048]{1,0:T(8,128)(2,1)}, u32[]{:S(2)}) copy-start(bf16[512,2048]{1,0:T(8,128)(2,1)} %all-gather.7.cloned.1.call-done) | copy-start | bytes 6291460
  157.0 99.9 %reduce-scatter.8.cloned.1.call-start = ((), (), s32[]{:S(2)}) async-start(), calls=%async_computation.9 | async-start | bytes 589824 | tf_op jit(solution)/shard_map/reduce_scatter | solution.py:86
  205.5 0.6 copy-start.5
  217.0 0.8 copy-start.2
  220.2 0.6 copy-start.7
  224.6 32.3 %copy-start.6 = (bf16[128,256]{1,0:T(8,128)(2,1)S(1)}, bf16[128,256]{1,0:T(8,128)(2,1)}, u32[]{:S(2)}) copy-start(bf16[128,256]{1,0:T(8,128)(2,1)} %copy-done.5) | copy-start | bytes 196612
  224.6 44.2 %copy-start.3 = (bf16[128,2048]{1,0:T(8,128)(2,1)S(1)}, bf16[128,2048]{1,0:T(8,128)(2,1)}, u32[]{:S(2)}) copy-start(bf16[128,2048]{1,0:T(8,128)(2,1)} %copy-done.2) | copy-start | bytes 1572868
  224.6 46.3 %all-to-all-start = ((bf16[2,128,2048]{1,0,2:T(2,128)(2,1)}), bf16[2,128,2048]{1,0,2:T(2,128)(2,1)S(1)}, u32[]{:S(2)}, u32[]{:S(2)}) async-start(bf16[2,128,2048]{1,0,2:T(2,128)(2,1)} %copy.11), calls=%async_computation.1 | async-start | bytes 2097152 | tf_op jit(solution)/shard_map/all_to_all | solution.py:101
  229.5 84.8 %all-gather.11.cloned.1.call-start = ((), (), s32[]{:S(2)}) async-start(), calls=%async_computation.11 | async-start | bytes 1310720 | tf_op jit(solution)/shard_map/all_gather | solution.py:97
  271.0 42.5 %all-to-all-start.1 = ((bf16[2,128,2048]{1,0,2:T(2,128)(2,1)}), bf16[2,128,2048]{1,0,2:T(2,128)(2,1)S(1)}, u32[]{:S(2)}, u32[]{:S(2)}) async-start(bf16[2,128,2048]{1,0,2:T(2,128)(2,1)} %copy.13), calls=%async_computation.4 | async-start | bytes 2097152 | tf_op jit(solution)/shard_map/all_to_all | solution.py:96
  275.6 2.5 copy-start.8
  275.6 50.7 %all-gather.9.cloned.1.call-start = ((), (), s32[]{:S(2)}) async-start(), calls=%async_computation.10 | async-start | bytes 1310720 | tf_op jit(solution)/shard_map/all_gather | solution.py:104
Sparse Core Ops, SparseCore 0:
  9.6 48.3 all-gather.4
  59.5 44.4 all-gather.6
  107.7 32.8 reduce-scatter.3
  157.1 34.0 reduce-scatter.5
  222.6 34.2 reduce-scatter.7
  258.4 37.5 all-gather.10
  297.5 28.6 all-gather.8
where the time goes:
time: 337 us; the launch traced here: 336 us
  waiting for transfers between devices  214 us (64%)
  blocking collectives  57.5 us (17%)
  matrix products  22.8 us (7%)
  between operations  14.3 us (4%)
  local copies, waits for them, and re-layouts  11 us (3%)
  starting transfers between devices  9.7 us (3%)
  other arithmetic  6.97 us (2%)
    reduce_scatter x2, waiting for transfers between devices, on_device(): lax.psum_scatter(partial_value.astype(jnp.bfloat16), 'col', scatter_dimen...  64.8 us
    all_gather x1, waiting for transfers between devices, on_device(): w_out_panel = lax.all_gather(w_out, 'row', axis=1, tiled=True)  44 us
    all_gather x1, waiting for transfers between devices, on_device(): w_in_panel = lax.all_gather(w_in, 'row', axis=0, tiled=True)  35.6 us
    all_to_all x1, waiting for transfers between devices, on_device(): lax.all_to_all(grad_stack, 'row', split_axis=2, concat_axis=1, tiled=True)  33.4 us
    reduce_scatter x1, waiting for transfers between devices, on_device(): lax.psum_scatter(input_part.astype(jnp.bfloat16), 'col', scatter_dimensio...  25.5 us
    all_gather x2, blocking collectives, on_device(): full_rows = lax.all_gather(current, 'col', axis=1, tiled=True)  23.6 us
    all_gather x2, blocking collectives, on_device(): grad_rows = lax.all_gather(state_grad, 'col', axis=1, tiled=True)  21.8 us
    psum x1, blocking collectives, shared_cosine(): lax.psum((jnp.sum(state_f * state_f, axis=-1), jnp.sum(state_f * target_f...  12.1 us
  transfers between devices with their start and end apart: 9, of which 7 were waited for; matrix products, arithmetic and copies ran while one was open for 6% of the time, Pallas kernels for 0%

commit v1 on v0

--- a/solution.py
+++ b/solution.py
@@ -41,7 +41,22 @@
     unroll_steps = targets.shape[0]
     col_width = state_start.shape[1]
     w_in_panel = lax.all_gather(w_in, "row", axis=0, tiled=True)
-    w_out_panel = lax.all_gather(w_out, "row", axis=1, tiled=True)
+    ways, here, step = (lax.axis_size("row"), lax.axis_index("row"), w_out.shape[1])
+    shape = [n * ways if d == 1 else n for d, n in enumerate(w_out.shape)]
+    w_out_panel = lax.dynamic_update_slice_in_dim(
+        jnp.zeros(shape, w_out.dtype), w_out, here * step, axis=1
+    )
+    going_up = going_down = w_out
+    for far in range(1, ways // 2 + 1):
+        going_up = lax.ppermute(going_up, "row", [(d, (d + 1) % ways) for d in range(ways)])
+        w_out_panel = lax.dynamic_update_slice_in_dim(
+            w_out_panel, going_up, (here - far) % ways * step, axis=1
+        )
+        if 2 * far < ways:
+            going_down = lax.ppermute(going_down, "row", [(d, (d - 1) % ways) for d in range(ways)])
+            w_out_panel = lax.dynamic_update_slice_in_dim(
+                w_out_panel, going_down, (here + far) % ways * step, axis=1
+            )
     col_start = lax.axis_index("col") * col_width
     action_ids = jnp.arange(action_embed.shape[0], dtype=jnp.int32)
     contract_last = (((1,), (1,)), ((), ()))

time: 337 us -> 315 us (0.935)
  waiting for transfers between devices: 214 us -> 181 us
  starting transfers between devices: 9.7 us -> 23.5 us
  blocking collectives: 57.5 us -> 53.3 us
    all_gather x1 -> x0, waiting for transfers between devices: 44 us -> none  [on_device(): w_out_panel = lax.all_gather(w_out, 'row', axis=1, tiled=True)]
    ppermute x0 -> x3, waiting for transfers between devices: none -> 37.8 us  [the longest x1 20.7 us: on_device(): lax.ppermute(going_down, 'row', [(d, (d - 1) % ways) for d in range(ways)])]
    all_gather x1, waiting for transfers between devices: 35.6 us -> 10 us  [on_device(): w_in_panel = lax.all_gather(w_in, 'row', axis=0, tiled=True)]
    ppermute x0 -> x3, starting transfers between devices: none -> 13.8 us  [the longest x2 11.7 us: on_device(): lax.ppermute(going_up, 'row', [(d, (d + 1) % ways) for d in range(ways)])]
    all_gather x2, blocking collectives: 23.6 us -> 19.5 us  [on_device(): full_rows = lax.all_gather(current, 'col', axis=1, tiled=True)]
  transfers between devices with their start and end apart: 9 -> 11, of which waited for: 7 -> 9; matrix products, arithmetic and copies ran while one was open for 6% -> 7% of each run, Pallas kernels for 0% -> 0%
where the time goes in v1:
time: 315 us; the launch traced here: 314 us
  waiting for transfers between devices  181 us (57%)
  blocking collectives  53.3 us (17%)
  starting transfers between devices  23.5 us (7%)
  matrix products  21.1 us (7%)
  between operations  14.3 us (5%)
  local copies, waits for them, and re-layouts  13.6 us (4%)
  other arithmetic  6.96 us (2%)
    reduce_scatter x2, waiting for transfers between devices, on_device(): lax.psum_scatter(partial_value.astype(jnp.bfloat16), 'col', scatter_dimen...  64.9 us
    all_to_all x1, waiting for transfers between devices, on_device(): lax.all_to_all(grad_stack, 'row', split_axis=2, concat_axis=1, tiled=True)  33.8 us
    reduce_scatter x1, waiting for transfers between devices, on_device(): lax.psum_scatter(input_part.astype(jnp.bfloat16), 'col', scatter_dimensio...  25.5 us
    all_gather x2, blocking collectives, on_device(): grad_rows = lax.all_gather(state_grad, 'col', axis=1, tiled=True)  21.7 us
    ppermute x1, waiting for transfers between devices, on_device(): lax.ppermute(going_down, 'row', [(d, (d - 1) % ways) for d in range(ways)])  20.7 us
    all_gather x2, blocking collectives, on_device(): full_rows = lax.all_gather(current, 'col', axis=1, tiled=True)  19.5 us
    ppermute x2, waiting for transfers between devices, on_device(): lax.ppermute(going_up, 'row', [(d, (d + 1) % ways) for d in range(ways)])  17.1 us
    psum x1, blocking collectives, shared_cosine(): lax.psum((jnp.sum(state_f * state_f, axis=-1), jnp.sum(state_f * target_f...  12.2 us
  transfers between devices with their start and end apart: 11, of which 9 were waited for; matrix products, arithmetic and copies ran while one was open for 7% of the time, Pallas kernels for 0%

profile of v1, /device:TPU:0, one launch (start us, length us, event | category | flops | bytes accessed | tf_op | source)
XLA Modules:
  0.0 314.3 jit_solution(18094225277210010467)
XLA Ops:
  8.0 3.1 collective-permute-start
  14.3 13.5 %collective-permute-done = bf16[512,512]{1,0:T(8,128)(2,1)} collective-permute-done((bf16[512,512]{1,0:T(8,128)(2,1)}, bf16[512,512]{1,0:T(8,128)(2,1)}, u32[]{:S(2)}, u32[]{:S(2)}) %collective-permute-start) | collective-permute-done | bytes 524320 | tf_op jit(solution)/shard_map/ppermute | solution.py:51
  27.8 8.6 %collective-permute-start.2 = (bf16[512,512]{1,0:T(8,128)(2,1)}, bf16[512,512]{1,0:T(8,128)(2,1)S(1)}, u32[]{:S(2)}, u32[]{:S(2)}) collective-permute-start(bf16[512,512]{1,0:T(8,128)(2,1)} %collective-permute-done), channel_id=1, source_target_pairs={{0,8},{8,16},{16,24},{24,0},{1,9},{9,17},{17,25},{25,1},{2,10},{10... | collective-permute-start | bytes 1572872 | tf_op jit(solution)/shard_map/ppermute | solution.py:51
  36.4 8.6 %all_gather.21 = bf16[128,2048]{1,0:T(8,128)(2,1)S(1)} all-gather(bf16[128,256]{1,0:T(8,128)(2,1)S(1)} %copy-done.12), channel_id=1, replica_groups=mesh['row'=4,'col'=8] {'col'}, dimensions={1}, use_global_device_ids=true | all-gather | bytes 589824 | tf_op jit(solution)/shard_map/all_gather | solution.py:69
  46.3 20.7 %collective-permute-done.1 = bf16[512,512]{1,0:T(8,128)(2,1)} collective-permute-done((bf16[512,512]{1,0:T(8,128)(2,1)}, bf16[512,512]{1,0:T(8,128)(2,1)}, u32[]{:S(2)}, u32[]{:S(2)}) %collective-permute-start.1) | collective-permute-done | bytes 524320 | tf_op jit(solution)/shard_map/ppermute | solution.py:56
  68.2 3.6 %collective-permute-done.2 = bf16[512,512]{1,0:T(8,128)(2,1)S(1)} collective-permute-done((bf16[512,512]{1,0:T(8,128)(2,1)}, bf16[512,512]{1,0:T(8,128)(2,1)S(1)}, u32[]{:S(2)}, u32[]{:S(2)}) %collective-permute-start.2) | collective-permute-done | bytes 524320 | tf_op jit(solution)/shard_map/ppermute | solution.py:51
  71.8 10.0 %all-gather.4.cloned.1.call-done = bf16[2048,512]{1,0:T(8,128)(2,1)} async-done(((bf16[512,512]{1,0:T(8,128)(2,1)}), bf16[2048,512]{1,0:T(8,128)(2,1)}) %all-gather.4.cloned.1.call-update) | async-done | bytes 2097168 | tf_op jit(solution)/shard_map/all_gather | solution.py:43
  88.3 30.7 %reduce-scatter.4.cloned.1.call-done = bf16[128,256]{1,0:T(8,128)(2,1)} async-done(((bf16[128,2048]{1,0:T(8,128)(2,1)}), bf16[128,256]{1,0:T(8,128)(2,1)}) %reduce-scatter.4.cloned.1.call-update) | async-done | bytes 65552 | tf_op jit(solution)/shard_map/reduce_scatter | solution.py:77
  120.1 10.9 %all_gather.23 = bf16[128,2048]{1,0:T(8,128)(2,1)S(1)} all-gather(bf16[128,256]{1,0:T(8,128)(2,1)S(1)} %get-tuple-element.14), channel_id=1, replica_groups=mesh['row'=4,'col'=8] {'col'}, dimensions={1}, use_global_device_ids=true | all-gather | bytes 589824 | tf_op jit(solution)/shard_map/all_gather | solution.py:69
  131.0 2.1 convolution_add_fusion
  133.1 2.2 convolution_convert_fusion.1
  135.4 34.2 %reduce-scatter.6.cloned.1.call-done = bf16[128,256]{1,0:T(8,128)(2,1)} async-done(((bf16[128,2048]{1,0:T(8,128)(2,1)}), bf16[128,256]{1,0:T(8,128)(2,1)}) %reduce-scatter.6.cloned.1.call-update) | async-done | bytes 65552 | tf_op jit(solution)/shard_map/reduce_scatter | solution.py:77
  170.7 12.2 %all-reduce = (f32[128]{0:T(128)S(1)}, f32[128]{0:T(128)S(1)}, f32[128]{0:T(128)S(1)}, f32[128]{0:T(128)S(1)}, f32[128]{0:T(128)S(1)}, /*index=5*/f32[128]{0:T(128)S(1)}) all-reduce(f32[128]{0:T(128)S(1)} %get-tuple-element.5, f32[128]{0:T(128)S(1)} %get-tuple-element.6, ...), channel_id=1, replica_groups=mesh['row'=4,'col'=8] {'col'}, use_global_device_ids=true, to_apply=%region_7.8 | all-reduce | flops 768 | bytes 6144 | tf_op jit(solution)/shard_map/psum | solution.py:27
  184.5 10.8 %all_gather.24 = bf16[128,2048]{1,0:T(8,128)(2,1)S(1)} all-gather(bf16[128,256]{1,0:T(8,128)(2,1)S(1)} %fusion.8), channel_id=1, replica_groups=mesh['row'=4,'col'=8] {'col'}, dimensions={1}, use_global_device_ids=true | all-gather | bytes 589824 | tf_op jit(solution)/shard_map/all_gather | solution.py:90
  196.1 2.4 fusion
  202.9 4.9 %all-to-all-start = ((bf16[2,128,2048]{1,0,2:T(2,128)(2,1)}), bf16[2,128,2048]{1,0,2:T(2,128)(2,1)S(1)}, u32[]{:S(2)}, u32[]{:S(2)}) async-start(bf16[2,128,2048]{1,0,2:T(2,128)(2,1)} %copy.11), calls=%async_computation.1 | async-start | bytes 2097152 | tf_op jit(solution)/shard_map/all_to_all | solution.py:116
  209.8 25.5 %reduce-scatter.8.cloned.1.call-done = bf16[128,256]{1,0:T(8,128)(2,1)} async-done(((bf16[128,2048]{1,0:T(8,128)(2,1)}), bf16[128,256]{1,0:T(8,128)(2,1)}) %reduce-scatter.8.cloned.1.call-update) | async-done | bytes 65552 | tf_op jit(solution)/shard_map/reduce_scatter | solution.py:101
  236.3 10.9 %all_gather.25 = bf16[128,2048]{1,0:T(8,128)(2,1)S(1)} all-gather(bf16[128,256]{1,0:T(8,128)(2,1)S(1)} %fusion.16), channel_id=1, replica_groups=mesh['row'=4,'col'=8] {'col'}, dimensions={1}, use_global_device_ids=true | all-gather | bytes 589824 | tf_op jit(solution)/shard_map/all_gather | solution.py:90
  249.3 4.6 %all-to-all-start.1 = ((bf16[2,128,2048]{1,0,2:T(2,128)(2,1)}), bf16[2,128,2048]{1,0,2:T(2,128)(2,1)S(1)}, u32[]{:S(2)}, u32[]{:S(2)}) async-start(bf16[2,128,2048]{1,0,2:T(2,128)(2,1)} %copy.13), calls=%async_computation.4 | async-start | bytes 2097152 | tf_op jit(solution)/shard_map/all_to_all | solution.py:111
  253.9 2.5 fusion.2
  258.4 33.8 %all-to-all-done.1 = bf16[2,128,2048]{1,0,2:T(2,128)(2,1)S(1)} async-done(((bf16[2,128,2048]{1,0,2:T(2,128)(2,1)}), bf16[2,128,2048]{1,0,2:T(2,128)(2,1)S(1)}, u32[]{:S(2)}, u32[]{:S(2)}) %all-to-all-start.1) | async-done | bytes 1048608 | tf_op jit(solution)/shard_map/all_to_all | solution.py:111
  293.1 2.9 convolution_bitcast_fusion
  296.0 8.5 %all-gather.6.cloned.1.call-done = bf16[2,512,512]{2,1,0:T(8,128)(2,1)} async-done(((bf16[2,128,512]{2,1,0:T(8,128)(2,1)}), bf16[2,512,512]{2,1,0:T(8,128)(2,1)}) %all-gather.6.cloned.1.call-update) | async-done | bytes 1048592 | tf_op jit(solution)/shard_map/all_gather | solution.py:119
  304.5 2.9 convolution_bitcast_fusion.1
  (70 shorter events, 29.6 us)
Async XLA Ops:
  7.2 37.8 %copy-start = (bf16[18,512]{1,0:T(8,128)(2,1)S(1)}, bf16[18,512]{1,0:T(8,128)(2,1)}, u32[]{:S(2)}) copy-start(bf16[18,512]{1,0:T(8,128)(2,1)} %param.11) | copy-start | bytes 55300
  7.2 7.0 %copy-start.9 = (bf16[512,512]{1,0:T(8,128)(2,1)S(1)}, bf16[512,512]{1,0:T(8,128)(2,1)}, u32[]{:S(2)}) copy-start(bf16[512,512]{1,0:T(8,128)(2,1)} %param.10) | copy-start | bytes 1572868
  7.2 29.2 %copy-start.12 = (bf16[128,256]{1,0:T(8,128)(2,1)S(1)}, bf16[128,256]{1,0:T(8,128)(2,1)}, u32[]{:S(2)}) copy-start(bf16[128,256]{1,0:T(8,128)(2,1)} %param.6) | copy-start | bytes 196612
  7.2 74.7 %all-gather.4.cloned.1.call-start = ((), (), s32[]{:S(2)}) async-start(), calls=%async_computation.5 | async-start | bytes 2621440 | tf_op jit(solution)/shard_map/all_gather | solution.py:43
  7.9 111.0 %reduce-scatter.4.cloned.1.call-start = ((), (), s32[]{:S(2)}) async-start(), calls=%async_computation.6 | async-start | bytes 589824 | tf_op jit(solution)/shard_map/reduce_scatter | solution.py:77
  8.0 19.8 %collective-permute-start = (bf16[512,512]{1,0:T(8,128)(2,1)}, bf16[512,512]{1,0:T(8,128)(2,1)}, u32[]{:S(2)}, u32[]{:S(2)}) collective-permute-start(bf16[512,512]{1,0:T(8,128)(2,1)} %param.10), channel_id=1, source_target_pairs={{0,8},{8,16},{16,24},{24,0},{1,9},{9,17},{17,25},{25,1},{2,10},{10... | collective-permute-start | bytes 1572872 | tf_op jit(solution)/shard_map/ppermute | solution.py:51
  11.1 56.0 %collective-permute-start.1 = (bf16[512,512]{1,0:T(8,128)(2,1)}, bf16[512,512]{1,0:T(8,128)(2,1)}, u32[]{:S(2)}, u32[]{:S(2)}) collective-permute-start(bf16[512,512]{1,0:T(8,128)(2,1)} %param.10), channel_id=1, source_target_pairs={{0,24},{8,0},{16,8},{24,16},{1,25},{9,1},{17,9},{25,17},{2,26},{10... | collective-permute-start | bytes 1572872 | tf_op jit(solution)/shard_map/ppermute | solution.py:56
  27.8 44.0 %collective-permute-start.2 = (bf16[512,512]{1,0:T(8,128)(2,1)}, bf16[512,512]{1,0:T(8,128)(2,1)S(1)}, u32[]{:S(2)}, u32[]{:S(2)}) collective-permute-start(bf16[512,512]{1,0:T(8,128)(2,1)} %collective-permute-done), channel_id=1, source_target_pairs={{0,8},{8,16},{16,24},{24,0},{1,9},{9,17},{17,25},{25,1},{2,10},{10... | collective-permute-start | bytes 1572872 | tf_op jit(solution)/shard_map/ppermute | solution.py:51
  71.8 12.1 %copy-start.2 = (bf16[512,2048]{1,0:T(8,128)(2,1)}, bf16[512,2048]{1,0:T(8,128)(2,1)S(1)}, u32[]{:S(2)}) copy-start(bf16[512,2048]{1,0:T(8,128)(2,1)S(1)} %constant_dynamic-update-slice_fusion) | copy-start | bytes 6291460
  85.2 45.8 %copy-start.1 = (bf16[2048,512]{1,0:T(8,128)(2,1)S(1)}, bf16[2048,512]{1,0:T(8,128)(2,1)}, u32[]{:S(2)}) copy-start(bf16[2048,512]{1,0:T(8,128)(2,1)} %all-gather.4.cloned.1.call-done) | copy-start | bytes 6291460
  85.2 84.4 %reduce-scatter.6.cloned.1.call-start = ((), (), s32[]{:S(2)}) async-start(), calls=%async_computation.7 | async-start | bytes 589824 | tf_op jit(solution)/shard_map/reduce_scatter | solution.py:77
  88.3 31.8 %copy-start.6 = (bf16[1,128,2048]{2,1,0:T(8,128)(2,1)}, bf16[1,128,2048]{2,1,0:T(8,128)(2,1)S(1)}, u32[]{:S(2)}) copy-start(bf16[1,128,2048]{2,1,0:T(8,128)(2,1)S(1)} %get-tuple-element.16) | copy-start | bytes 1572868
  119.0 14.2 %copy-start.3 = (bf16[512,2048]{1,0:T(8,128)(2,1)S(1)}, bf16[512,2048]{1,0:T(8,128)(2,1)}, u32[]{:S(2)}) copy-start(bf16[512,2048]{1,0:T(8,128)(2,1)} %copy-done.2) | copy-start | bytes 6291460
  135.3 99.9 %reduce-scatter.8.cloned.1.call-start = ((), (), s32[]{:S(2)}) async-start(), calls=%async_computation.8 | async-start | bytes 589824 | tf_op jit(solution)/shard_map/reduce_scatter | solution.py:101
  183.8 0.6 copy-start.7
  195.3 0.8 copy-start.4
  198.5 0.6 copy-start.10
  202.9 32.4 %copy-start.8 = (bf16[128,256]{1,0:T(8,128)(2,1)S(1)}, bf16[128,256]{1,0:T(8,128)(2,1)}, u32[]{:S(2)}) copy-start(bf16[128,256]{1,0:T(8,128)(2,1)} %copy-done.7) | copy-start | bytes 196612
  202.9 44.2 %copy-start.5 = (bf16[128,2048]{1,0:T(8,128)(2,1)S(1)}, bf16[128,2048]{1,0:T(8,128)(2,1)}, u32[]{:S(2)}) copy-start(bf16[128,2048]{1,0:T(8,128)(2,1)} %copy-done.4) | copy-start | bytes 1572868
  202.9 46.3 %all-to-all-start = ((bf16[2,128,2048]{1,0,2:T(2,128)(2,1)}), bf16[2,128,2048]{1,0,2:T(2,128)(2,1)S(1)}, u32[]{:S(2)}, u32[]{:S(2)}) async-start(bf16[2,128,2048]{1,0,2:T(2,128)(2,1)} %copy.11), calls=%async_computation.1 | async-start | bytes 2097152 | tf_op jit(solution)/shard_map/all_to_all | solution.py:116
  207.9 85.2 %all-gather.8.cloned.1.call-start = ((), (), s32[]{:S(2)}) async-start(), calls=%async_computation.10 | async-start | bytes 1310720 | tf_op jit(solution)/shard_map/all_gather | solution.py:112
  249.3 43.0 %all-to-all-start.1 = ((bf16[2,128,2048]{1,0,2:T(2,128)(2,1)}), bf16[2,128,2048]{1,0,2:T(2,128)(2,1)S(1)}, u32[]{:S(2)}, u32[]{:S(2)}) async-start(bf16[2,128,2048]{1,0,2:T(2,128)(2,1)} %copy.13), calls=%async_computation.4 | async-start | bytes 2097152 | tf_op jit(solution)/shard_map/all_to_all | solution.py:111
  253.9 2.5 copy-start.11
  253.9 50.6 %all-gather.6.cloned.1.call-start = ((), (), s32[]{:S(2)}) async-start(), calls=%async_computation.9 | async-start | bytes 1310720 | tf_op jit(solution)/shard_map/all_gather | solution.py:119
Sparse Core Ops, SparseCore 0:
  9.6 72.2 all-gather.3
  85.5 33.4 reduce-scatter.3
  135.5 34.1 reduce-scatter.5
  200.9 34.2 reduce-scatter.7
  236.7 37.5 all-gather.7
  275.7 28.8 all-gather.5
